TPU v7x, 32 devices: a whole 2x2x4 slice. The times are simulated.
32 devices in a mesh: batch: 2 (over y), seq: 16 (over z, x, core).
Axes of the slice: x: 2, y: 2, z: 4, core: 2. Of those that a mesh axis runs over, the one named last changes fastest.
Arguments:
- tokens: bfloat16 [32, 64, 32, 768], P('batch', None, 'seq'), may hold values from -6 to 6
- lengths: int32 [32], P('batch'), may hold values from 256 to 2048
- labels: int32 [32, 64, 32], P('batch', None, 'seq'), may hold values from 0 to 767
- picked: int32 [32, 64, 32], P('batch', None, 'seq'), may hold values 0 or 1
- cotangent: bfloat16 [32, 64, 32, 768], P('batch', None, 'seq'), may hold values from -6 to 6
- w_in: bfloat16 [1, 768, 3072], P(None, None, ('batch', 'seq')), may hold values from -0.21875 to 0.21875
- b_in: bfloat16 [1, 3072], P(None, ('batch', 'seq')), may hold values from -1.796875 to 1.796875
- w_out: bfloat16 [1, 3072, 768], P(None, ('batch', 'seq')), may hold values from -0.109375 to 0.109375
- shifts: bfloat16 [1, 3, 768], P(None, None, ('batch', 'seq')), may hold values from -1.796875 to 1.796875
- norm_gains: bfloat16 [1, 2, 768], P(None, None, ('batch', 'seq')), may hold values from 0.25 to 1.75
Outputs:
- mixed: bfloat16 [32, 64, 32, 768], P('batch', None, 'seq')
- input_grad: bfloat16 [32, 64, 32, 768], P('batch', None, 'seq')
- grad_w_in: float32 [1, 768, 3072], P(None, None, ('batch', 'seq'))
- grad_b_in: float32 [1, 3072], P(None, ('batch', 'seq'))
- grad_w_out: float32 [1, 3072, 768], P(None, ('batch', 'seq'))
- grad_shifts: float32 [1, 3, 768], P(None, None, ('batch', 'seq'))
- grad_gains: float32 [1, 2, 768], P(None, None, ('batch', 'seq'))
- match_rate: float32 [], replicated
All inputs are finite; a program needn't handle non-finite values. No bound on the sum of `picked` on one device may be relied on, other than what follows from the above.
Results may differ from a plain program's by a relative error of at most 0.0095.
Values may be sent and summed in bfloat16 or wider, within the bound.
No kernel may reach another device: no remote copies, remote signals or barrier semaphores. Data moves between devices by JAX's collectives and lax.ppermute only.
A program may use at most 192 MiB of HBM per device.

v0:
```python
import math
import jax
import jax.numpy as jnp
from jax import lax
from jax.sharding import PartitionSpec as P

D = 768
L1 = 64
L2 = 32
L = 2048
EPSILON = 1e-12
ROOT_TWO_PI = 0.7978845608028654
F32 = jnp.float32
BF16 = jnp.bfloat16


def layer_norm(values, gain_rows, shift_rows):
    center = values - jnp.mean(values, axis=-1, keepdims=True)
    spread = jnp.mean(center * center, axis=-1, keepdims=True)
    return center * lax.rsqrt(spread + EPSILON) * gain_rows + shift_rows


def gelu(values):
    return (
        0.5
        * values
        * (1.0 + jnp.tanh(ROOT_TWO_PI * (values + 0.044715 * values * values * values)))
    )


def table_pair(points):
    numbers = jnp.arange(points, dtype=jnp.int32)
    product_mod = numbers[:, None] * numbers[None, :] % points
    angles = product_mod.astype(F32) * (2.0 * math.pi / points)
    factor = 1.0 / math.sqrt(points)
    return ((jnp.cos(angles) * factor).astype(BF16), (jnp.sin(angles) * factor).astype(BF16))


def twiddles():
    row_index = jnp.arange(L1, dtype=jnp.int32)[None, :]
    col_index = jnp.arange(L2, dtype=jnp.int32)[:, None]
    angles = (row_index * col_index % L).astype(F32) * (2.0 * math.pi / L)
    return (jnp.cos(angles)[:, :, None], jnp.sin(angles)[:, :, None])


def swap(values, step):
    axis, mask = step
    size = lax.axis_size(axis)
    return lax.ppermute(values, axis, [(i, i ^ mask) for i in range(size)])


def bits(size):
    masks = []
    mask = size // 2
    while mask >= 1:
        masks.append(mask)
        mask //= 2
    return masks


def xor_gather(block, steps):
    held = block[None]
    for step in steps:
        held = jnp.concatenate([held, swap(held, step)], axis=0)
    return held


def xor_scatter(held, steps):
    for step in reversed(steps):
        half = held.shape[0] // 2
        arrived = swap(held[half:].astype(BF16), step)
        held = held[:half].astype(F32) + arrived.astype(F32)
    return held[0]


def body(tokens, lengths, labels, picked, cotangent, w_in, b_in, w_out, shifts, norm_gains):
    groups = lax.axis_size("seq")
    me = lax.axis_index("seq")
    columns = tokens.shape[2]
    share = w_in.shape[2]
    steps = (
        [("seq", mask) for mask in bits(groups)[:-1]]
        + [("batch", mask) for mask in bits(lax.axis_size("batch"))]
        + [("seq", 1)]
    )
    early = len(bits(groups)) - 1
    own = jnp.stack([w_in[0].T, w_out[0]])
    held = own[None]
    for step in steps[: early - 1]:
        held = jnp.concatenate([held, swap(held, step)], axis=0)
    tokens_late, held = lax.optimization_barrier((tokens, held))
    for step in steps[early - 1 :]:
        held = jnp.concatenate([held, swap(held, step)], axis=0)
    hidden_units = held.shape[0] * share
    w_first = held[:, 0].reshape(hidden_units, D)
    w_second = held[:, 1].reshape(hidden_units, D)
    packed = jnp.concatenate([shifts[0].reshape(-1), norm_gains[0].reshape(-1)])
    packed = lax.all_gather(packed, ("batch", "seq"), axis=0)
    rows = packed.reshape(packed.shape[0], 5, -1).transpose(1, 0, 2).reshape(5, D)
    shifts_f = rows[:3].astype(F32)
    gains_f = rows[3:].astype(F32)
    b_first = xor_gather(b_in[0].astype(F32), steps).reshape(hidden_units)
    short_cos, short_sin = table_pair(L1)
    long_cos, long_sin = table_pair(L2)
    wide_cos, wide_sin = table_pair(D)
    short_table = jnp.concatenate([short_cos, short_sin], axis=0)
    long_table = jnp.stack([jnp.stack([long_cos, -long_sin]), jnp.stack([long_sin, long_cos])])
    both = jnp.eye(2, dtype=BF16)
    pair_table = jnp.einsum("qukm,bc->qkbcum", long_table, both).reshape(4 * L2, 4 * L2)
    wide = jnp.stack([wide_cos, -wide_sin])
    twiddle_cos, twiddle_sin = twiddles()
    x_all = lax.all_to_all(tokens_late, "seq", split_axis=0, concat_axis=0, tiled=True)
    x_all, late_cotangent = lax.optimization_barrier((x_all, cotangent))
    g_all = lax.all_to_all(late_cotangent, "seq", split_axis=0, concat_axis=0, tiled=True)
    length = lengths[me]
    spots = L2 * jnp.arange(L1, dtype=jnp.int32)[None, :] + jnp.arange(L2, dtype=jnp.int32)[:, None]
    x_rows = x_all.transpose(0, 2, 1, 3).reshape(L2, L1, D)
    x_rows = jnp.where((spots < length)[:, :, None], x_rows, jnp.zeros_like(x_rows))
    first = jnp.einsum("kn,mnd->mkd", short_table, x_rows, preferred_element_type=F32)
    first_cos, first_sin = (first[:, :L1], first[:, L1:])
    turned_cos = (first_cos * twiddle_cos - first_sin * twiddle_sin).astype(BF16)
    turned_sin = (first_cos * twiddle_sin + first_sin * twiddle_cos).astype(BF16)
    turned = jnp.stack([turned_cos, turned_sin]).reshape(2, L2, 2, L2, D)
    turned = turned.transpose(3, 2, 0, 1, 4).reshape(L2, 4 * L2, D)
    spectrum = jnp.einsum("rk,lkd->lrd", pair_table, turned, preferred_element_type=F32)
    spectrum = spectrum.astype(BF16).reshape(L2, 2, L1, D)
    mixed = jnp.einsum("lund,ude->lne", spectrum, wide, preferred_element_type=F32)
    residual = (x_rows.astype(F32) + mixed).reshape(L, D)
    normed = layer_norm(residual, gains_f[0], shifts_f[1])
    normed_low = normed.astype(BF16)
    pre_act = jnp.einsum("td,fd->tf", normed_low, w_first, preferred_element_type=F32) + b_first
    act_low = gelu(pre_act).astype(BF16)
    summed = normed + jnp.dot(act_low, w_second, preferred_element_type=F32) + shifts_f[0]
    layer_out = layer_norm(summed, gains_f[1], shifts_f[2]).astype(BF16)
    out_rows = layer_out.reshape(groups, columns, L1, D)
    out_rows = lax.all_to_all(out_rows, "seq", split_axis=0, concat_axis=0, tiled=True)
    current = out_rows.transpose(0, 2, 1, 3)
    grad_out = g_all.transpose(0, 2, 1, 3).reshape(L, D).astype(F32)
    unused, pull_second = jax.vjp(layer_norm, summed, gains_f[1], shifts_f[2])
    grad_summed, grad_gain_two, grad_shift_two = pull_second(grad_out)
    grad_bias_two = jnp.sum(grad_summed, axis=0)
    summed_low = grad_summed.astype(BF16)
    grad_w_second = jnp.einsum("tf,td->fd", act_low, summed_low, preferred_element_type=F32)
    grad_act = jnp.einsum("td,fd->tf", summed_low, w_second, preferred_element_type=F32)
    unused_act, pull_gelu = jax.vjp(gelu, pre_act)
    grad_pre = pull_gelu(grad_act)[0]
    grad_b_first = jnp.sum(grad_pre, axis=0)
    pre_low = grad_pre.astype(BF16)
    grad_w_first = jnp.einsum("tf,td->fd", pre_low, normed_low, preferred_element_type=F32)
    grad_normed = grad_summed + jnp.dot(pre_low, w_first, preferred_element_type=F32)
    normed_again, pull_first = jax.vjp(layer_norm, residual, gains_f[0], shifts_f[1])
    grad_residual, grad_gain_one, grad_shift_one = pull_first(grad_normed)
    residual_low = grad_residual.astype(BF16).reshape(L2, L1, D)
    grad_spectrum = jnp.einsum("lne,ude->lund", residual_low, wide, preferred_element_type=F32)
    grad_spectrum = grad_spectrum.astype(BF16).reshape(L2, 4 * L2, D)
    grad_turned = jnp.einsum("rk,lrd->lkd", pair_table, grad_spectrum, preferred_element_type=F32)
    grad_turned = grad_turned.astype(BF16).reshape(L2, 2, 2, L2, D).transpose(2, 3, 1, 0, 4)
    grad_turned = grad_turned.reshape(2, L2, L1, D)
    grad_cos, grad_sin = (grad_turned[0], grad_turned[1])
    back_cos = grad_cos * twiddle_cos + grad_sin * twiddle_sin
    back_sin = grad_sin * twiddle_cos - grad_cos * twiddle_sin
    stacked = jnp.concatenate([back_cos, back_sin], axis=1).astype(BF16)
    grad_x = residual_low.astype(F32) + jnp.einsum(
        "kn,mkd->mnd", short_table, stacked, preferred_element_type=F32
    )
    grad_x = jnp.where((spots < length)[:, :, None], grad_x, 0.0).astype(BF16)
    grad_x = grad_x.reshape(groups, columns, L1, D)
    grad_x = lax.all_to_all(grad_x, "seq", split_axis=0, concat_axis=0, tiled=True)
    input_grad = grad_x.transpose(0, 2, 1, 3)
    grad_first = xor_scatter(grad_w_first.reshape(-1, share, D), steps)
    grad_second = xor_scatter(grad_w_second.reshape(-1, share, D), steps)
    hidden_total = hidden_units
    here = lax.axis_index("batch") * groups + me
    blocks = grad_b_first.reshape(-1, share)
    block_of = []
    for number in range(blocks.shape[0]):
        code_seq, code_batch = (0, 0)
        for place, (axis, mask) in enumerate(steps):
            if number >> place & 1:
                if axis == "seq":
                    code_seq ^= mask
                else:
                    code_batch ^= mask
        block_of.append(code_batch * groups + code_seq)
    owner = jnp.array(block_of, dtype=jnp.int32) ^ here
    one_hot = (owner[None, :] == jnp.arange(blocks.shape[0], dtype=jnp.int32)[:, None]).astype(F32)
    ordered = jnp.sum(one_hot[:, :, None] * blocks[None], axis=1).reshape(hidden_total // D, D)
    shift_of = jnp.arange(columns, dtype=jnp.int32) + me * columns
    place_of = L2 * jnp.arange(L1, dtype=jnp.int32)[:, None] + shift_of[None, :]
    valid_mask = place_of[None] < lengths[:, None, None]
    logits = out_rows.astype(F32)
    label_rows = labels.transpose(0, 2, 1)
    highest = jnp.max(logits, axis=-1)
    powers = jnp.exp(logits - highest[..., None])
    denominator = jnp.sum(powers, axis=-1)
    features = jnp.arange(D, dtype=jnp.int32)
    top = jnp.sum(jnp.where(features == label_rows[..., None], powers, 0.0), axis=-1)
    chance = top / denominator
    weight = (picked.astype(F32) * valid_mask.astype(F32)).transpose(0, 2, 1)
    sums = jnp.stack([jnp.sum(weight * chance), jnp.sum(weight)])
    sums = jnp.pad(sums, (0, D - 2))[None]
    rest = jnp.concatenate(
        [
            jnp.stack(
                [grad_bias_two, grad_shift_one, grad_shift_two, grad_gain_one, grad_gain_two]
            ),
            ordered,
            sums,
        ]
    )
    rest = lax.psum(rest, ("batch", "seq"))
    slice_of = D // (lax.axis_size("batch") * groups)
    norms = lax.dynamic_slice_in_dim(rest[:5], here * slice_of, slice_of, axis=1)
    grad_b_in = lax.dynamic_slice_in_dim(rest[5:-1].reshape(-1), here * share, share, axis=0)
    match_rate = D * rest[-1, 0] / jnp.maximum(rest[-1, 1], 1.0)
    return (
        current,
        input_grad,
        grad_first.T[None],
        grad_b_in[None],
        grad_second[None],
        norms[:3][None],
        norms[3:][None],
        match_rate,
    )


def solution(mesh):
    in_specs = (
        P("batch", None, "seq", None),
        P("batch"),
        P("batch", None, "seq"),
        P("batch", None, "seq"),
        P("batch", None, "seq", None),
        P(None, None, ("batch", "seq")),
        P(None, ("batch", "seq")),
        P(None, ("batch", "seq"), None),
        P(None, None, ("batch", "seq")),
        P(None, None, ("batch", "seq")),
    )
    out_specs = (
        P("batch", None, "seq", None),
        P("batch", None, "seq", None),
        P(None, None, ("batch", "seq")),
        P(None, ("batch", "seq")),
        P(None, ("batch", "seq"), None),
        P(None, None, ("batch", "seq")),
        P(None, None, ("batch", "seq")),
        P(),
    )
    return jax.shard_map(body, mesh=mesh, in_specs=in_specs, out_specs=out_specs, check_vma=False)
```

profile of v0, /device:TPU:0, one launch (start us, length us, event | category | flops | bytes accessed | tf_op | source)
XLA Modules:
  0.0 656.5 jit_solution(15531649239720909190)
XLA Ops:
  5.8 13.3 %collective-permute-done = bf16[1,2,96,768]{3,2,1,0:T(8,128)(2,1)S(1)} collective-permute-done((bf16[1,2,96,768]{3,2,1,0:T(8,128)(2,1)S(1)}, bf16[1,2,96,768]{3,2,1,0:T(8,128)(2,1)S(1)}, u32[]{:S(2)}, u32[]{:S(2)}) %collective-permute-start) | collective-permute-done | bytes 294944 | tf_op jit(solution)/shard_map/ppermute | solution.py:49
  20.0 13.8 %collective-permute-done.1 = bf16[2,2,96,768]{3,2,1,0:T(8,128)(2,1)S(1)} collective-permute-done((bf16[2,2,96,768]{3,2,1,0:T(8,128)(2,1)S(1)}, bf16[2,2,96,768]{3,2,1,0:T(8,128)(2,1)S(1)}, u32[]{:S(2)}, u32[]{:S(2)}) %collective-permute-start.1) | collective-permute-done | bytes 589856 | tf_op jit(solution)/shard_map/ppermute | solution.py:49
  33.9 6.6 %all-to-all-start = ((bf16[16,64,2,768]{3,2,1,0:T(2,128)(2,1)}), bf16[16,64,2,768]{3,2,1,0:T(2,128)(2,1)}, u32[]{:S(2)}, u32[]{:S(2)}) async-start(bf16[16,64,2,768]{3,2,1,0:T(2,128)(2,1)} %param.11), calls=%async_computation | async-start | bytes 6291456 | tf_op jit(solution)/shard_map/all_to_all | solution.py:112
  47.2 55.5 %collective-permute-done.2 = bf16[4,2,96,768]{3,2,1,0:T(8,128)(2,1)S(1)} collective-permute-done((bf16[4,2,96,768]{3,2,1,0:T(8,128)(2,1)S(1)}, bf16[4,2,96,768]{3,2,1,0:T(8,128)(2,1)S(1)}, u32[]{:S(2)}, u32[]{:S(2)}) %collective-permute-start.2) | collective-permute-done | bytes 1179680 | tf_op jit(solution)/shard_map/ppermute | solution.py:49
  106.1 83.7 %all-reduce.1 = bf16[3840]{0:T(1024)(128)(2,1)S(1)} all-reduce(bf16[3840]{0:T(1024)(128)(2,1)S(1)} %dynamic-update-slice), channel_id=2, replica_groups=mesh['batch'=2,'seq'=16] {'batch','seq'}, use_global_device_ids=true, to_apply=%add.1 | all-reduce | flops 3840 | bytes 15360
  190.8 10.0 %fusion.34 = bf16[1,768,768]{2,1,0:T(8,128)(2,1)} fusion(), kind=kLoop, calls=%fused_computation.87 | loop fusion | flops 8257536 | bytes 1179648 | tf_op jit(solution)/shard_map/neg | solution.py:110
  200.9 9.9 %multiply_convert_fusion.2 = bf16[1,768,768]{2,1,0:T(8,128)(2,1)} fusion(), kind=kLoop, calls=%fused_computation.82 | loop fusion | flops 6488064 | bytes 1179648 | tf_op jit(solution)/shard_map/convert_element_type | solution.py:36
  235.1 5.8 all-to-all-start.2
  252.7 7.2 %fusion.73 = (f32[32,64]{1,0:T(8,128)S(1)}, f32[32,64,768]{2,1,0:T(8,128)}) fusion(bf16[32,2,64,768]{3,2,1,0:T(8,128)(2,1)S(1)} %bitcast.161, bf16[1,768,768]{2,1,0:T(8,128)(2,1)S(1)} %copy-done.10, bf16[1,768,768]{2,1,0:T(8,128)(2,1)S(1)} %copy-done.12, bf16[32,64,768]{2,1,0:T(8,128)(2,1)S(1)} %bitcast_select_fusion), kind=kOutput, calls=%fused_computation.198 | convolution fusion | flops 4837734400 | bytes 18096128 | tf_op jit(solution)/shard_map/lund,ude->lne/dot_general | solution.py:127
  268.4 5.0 constant_dynamic-update-slice_fusion
  273.4 8.0 %fusion.70 = (bf16[32,1,96,768]{3,2,1,0:T(8,128)(2,1)}, bf16[32,1,96,768]{3,2,1,0:T(8,128)(2,1)}) fusion(bf16[32,2,96,768]{3,2,1,0:T(8,128)(2,1)} %constant_dynamic-update-slice_fusion), kind=kLoop, calls=%fused_computation.195 | loop fusion | bytes 18874368 | tf_op jit(solution)/shard_map/slice | solution.py:96
  281.4 24.9 %multiply_convert_fusion = (bf16[2048,3072]{1,0:T(8,128)(2,1)}, f32[2048,3072]{1,0:T(8,128)}) fusion(f32[3072]{0:T(1024)S(1)} %add.303, bf16[2048,768]{1,0:T(8,128)(2,1)} %bitcast.169, bf16[3072,768]{1,0:T(8,128)(2,1)} %bitcast.162), kind=kOutput, calls=%fused_computation.9 | convolution fusion | flops 9726590976 | bytes 45625344 | tf_op jit(solution)/shard_map/td,fd->tf/dot_general | solution.py:131
  306.3 16.2 %fusion.74 = (f32[2048]{0:T(1024)S(1)}, f32[2048,768]{1,0:T(8,128)S(1)}) fusion(f32[768]{0:T(1024)S(1)} %add.309, bf16[2048,3072]{1,0:T(8,128)(2,1)} %get-tuple-element.82, bf16[3072,768]{1,0:T(8,128)(2,1)} %bitcast.164, f32[768]{0:T(1024)S(1)} %add.298, f32[768]{0:T(1024)S(1)} %mul.622, f32[2048]{0:T(1024)S(1)} %rsqrt.25, f32[2048]{0:T(1024)S(1)} %div.52, ...), kind=kOutput, calls=%fused_computation.199 | convolution fusion | flops 9674684416 | bytes 29918208 | tf_op jit(solution)/shard_map/dot_general | solution.py:133
  338.3 17.8 %fusion.67 = f32[3072,768]{1,0:T(8,128)} fusion(bf16[2048,3072]{1,0:T(8,128)(2,1)} %get-tuple-element.82, f32[2048,768]{1,0:T(8,128)S(1)} %get-tuple-element.63, f32[2048]{0:T(1024)S(1)} %negate_multiply_fusion.1), kind=kOutput, calls=%fused_computation.192 | convolution fusion | flops 9666822144 | bytes 28319744 | tf_op jit(solution)/shard_map/tf,td->fd/dot_general | solution.py:143
  356.1 34.4 %fusion.75 = (f32[3072]{0:T(1024)S(1)}, bf16[2048,3072]{1,0:T(8,128)(2,1)}) fusion(bf16[3072,768]{1,0:T(8,128)(2,1)} %bitcast.165, f32[2048,768]{1,0:T(8,128)S(1)} %get-tuple-element.63, f32[2048]{0:T(1024)S(1)} %negate_multiply_fusion.1, f32[2048,3072]{1,0:T(8,128)} %get-tuple-element.83, f32[3072]{0:T(1024)S(1)} %add.303), kind=kOutput, calls=%fused_computation.200 | convolution fusion | flops 9830396928 | bytes 48791552 | tf_op jit(solution)/shard_map/td,fd->tf/dot_general | solution.py:144
  390.5 6.8 %copy.55 = bf16[16,2,64,768]{3,1,2,0:T(2,128)(2,1)} copy(bf16[16,2,64,768]{3,2,1,0:T(8,128)(2,1)} %bitcast.156) | data formatting | bytes 6291456 | tf_op jit(solution)/shard_map/reshape | solution.py:135
  397.4 17.3 %multiply_reduce_fusion = (f32[768]{0:T(1024)S(1)}, f32[2048]{0:T(1024)S(1)}, f32[768]{0:T(1024)S(1)}, f32[2048,768]{1,0:T(8,128)}) fusion(f32[32,64,768]{2,1,0:T(8,128)S(1)} %bitcast.144, f32[2048]{0:T(1024)S(1)} %rsqrt.25, f32[2048]{0:T(1024)S(1)} %div.52, f32[768]{0:T(1024)S(1)} %mul.622, bf16[3072,768]{1,0:T(8,128)(2,1)} %bitcast.163, ...), kind=kOutput, calls=%fused_computation.39 | convolution fusion | flops 9679400960 | bytes 36217856 | tf_op jit(solution)/shard_map/dot_general | solution.py:150
  414.7 6.5 all-to-all-start.1
  421.2 7.2 %fusion.68 = (f32[2048]{0:T(1024)S(1)}, f32[2048,768]{1,0:T(8,128)S(1)}, bf16[2048,768]{1,0:T(8,128)(2,1)}) fusion(f32[2048]{0:T(1024)S(1)} %multiply_multiply_fusion.2, f32[2048]{0:T(1024)S(1)} %div.52, f32[32,64,768]{2,1,0:T(8,128)} %get-tuple-element.81, f32[2048]{0:T(1024)S(1)} %rsqrt.25, f32[2048,768]{1,0:T(8,128)} %get-tuple-element.86, ...), kind=kLoop, calls=%fused_computation.193 | loop fusion | flops 17299456 | bytes 22059008 | tf_op jit(solution)/shard_map/transpose(jvp())/reduce_sum | solution.py:18
  428.5 14.2 %fusion.17 = f32[3072,768]{1,0:T(8,128)S(1)} fusion(bf16[2048,768]{1,0:T(8,128)(2,1)} %get-tuple-element.70, bf16[2048,3072]{1,0:T(8,128)(2,1)} %get-tuple-element.88), kind=kOutput, calls=%fused_computation.43 | convolution fusion | flops 9663676416 | bytes 25165824 | tf_op jit(solution)/shard_map/tf,td->fd/dot_general | solution.py:149
  448.9 8.9 %convert_bitcast_fusion.1 = bf16[32,2,64,768]{3,2,0,1:T(8,128)(2,1)} fusion(bf16[32,64,768,1]{2,1,0,3:T(8,128)(2,1)} %bitcast.167, bf16[1,768,768]{2,1,0:T(8,128)(2,1)S(1)} %copy-done.11, bf16[1,768,768]{2,1,0:T(8,128)(2,1)} %multiply_convert_fusion.2), kind=kOutput, calls=%fused_computation.40 | convolution fusion | flops 4839702528 | bytes 11796480 | tf_op jit(solution)/shard_map/lne,ude->lund/dot_general | solution.py:154
  481.5 4.9 copy.60
  486.4 9.9 %all-to-all-start.3 = ((bf16[16,2,64,768]{3,1,2,0:T(2,128)(2,1)}), bf16[16,2,64,768]{3,1,2,0:T(2,128)(2,1)}, u32[]{:S(2)}, u32[]{:S(2)}) async-start(bf16[16,2,64,768]{3,1,2,0:T(2,128)(2,1)} %copy.60), calls=%async_computation.3 | async-start | bytes 6291456 | tf_op jit(solution)/shard_map/all_to_all | solution.py:168
  508.4 19.2 %collective-permute-done.11 = bf16[8,96,768]{2,1,0:T(8,128)(2,1)} collective-permute-done((bf16[8,96,768]{2,1,0:T(8,128)(2,1)}, bf16[8,96,768]{2,1,0:T(8,128)(2,1)}, u32[]{:S(2)}, u32[]{:S(2)}) %collective-permute-start.11) | collective-permute-done | bytes 1179680 | tf_op jit(solution)/shard_map/ppermute | solution.py:49
  532.2 5.6 collective-permute-done.17
  538.7 19.7 %collective-permute-done.12 = bf16[4,96,768]{2,1,0:T(8,128)(2,1)S(1)} collective-permute-done((bf16[4,96,768]{2,1,0:T(8,128)(2,1)S(1)}, bf16[4,96,768]{2,1,0:T(8,128)(2,1)S(1)}, u32[]{:S(2)}, u32[]{:S(2)}) %collective-permute-start.12) | collective-permute-done | bytes 589856 | tf_op jit(solution)/shard_map/ppermute | solution.py:49
  561.3 7.2 %collective-permute-done.13 = bf16[2,96,768]{2,1,0:T(8,128)(2,1)} collective-permute-done((bf16[2,96,768]{2,1,0:T(8,128)(2,1)}, bf16[2,96,768]{2,1,0:T(8,128)(2,1)}, u32[]{:S(2)}, u32[]{:S(2)}) %collective-permute-start.13) | collective-permute-done | bytes 294944 | tf_op jit(solution)/shard_map/ppermute | solution.py:49
  569.7 8.5 %collective-permute-start.14 = (bf16[1,96,768]{2,1,0:T(8,128)(2,1)S(1)}, bf16[1,96,768]{2,1,0:T(8,128)(2,1)S(1)}, u32[]{:S(2)}, u32[]{:S(2)}) collective-permute-start(bf16[1,96,768]{2,1,0:T(8,128)(2,1)S(1)} %slice.266), channel_id=1, source_target_pairs={{0,8},{1,9},{2,10},{3,11},{4,12},{5,13},{6,14},{7,15},{8,0},{9,1},... | collective-permute-start | bytes 442376 | tf_op jit(solution)/shard_map/ppermute | solution.py:49
  579.0 6.4 collective-permute-done.14
  588.7 13.2 %fusion.22 = (f32[16,2,64]{1,2,0:T(8,128)S(1)}, f32[16,2,64]{1,2,0:T(8,128)S(1)}) fusion(bf16[16,2,64,768]{3,1,2,0:T(2,128)(2,1)S(1)} %all-to-all-done.1, f32[16,2,64]{1,2,0:T(8,128)S(1)} %reduce_max.15, s32[16,2,64]{1,2,0:T(8,128)} %copy.62), kind=kLoop, calls=%fused_computation.60 | loop fusion | flops 9433088 | bytes 3178496 | tf_op jit(solution)/shard_map/reduce_sum | solution.py:195
  604.3 39.5 %psum.7 = f32[10,768]{1,0:T(8,128)S(1)} all-reduce(f32[10,768]{1,0:T(8,128)S(1)} %concatenate.64), channel_id=1, replica_groups=mesh['batch'=2,'seq'=16] {'batch','seq'}, use_global_device_ids=true, to_apply=%region_20.21 | all-reduce | flops 7680 | bytes 61440 | tf_op jit(solution)/shard_map/psum | solution.py:211
  649.3 5.9 copy.77
  (264 shorter events, 139.1 us)
Async XLA Ops:
  0.6 45.3 %copy-start.36 = (s32[32]{0:T(128)S(1)}, s32[32]{0:T(128)}, u32[]{:S(2)}) copy-start(s32[32]{0:T(128)} %constant.129.clone) | copy-start | bytes 388
  0.7 42.8 %copy-start.34 = (bf16[1,3,24]{2,1,0:T(4,128)(2,1)S(1)}, bf16[1,3,24]{2,1,0:T(4,128)(2,1)}, u32[]{:S(2)}) copy-start(bf16[1,3,24]{2,1,0:T(4,128)(2,1)} %param.19) | copy-start | bytes 436
  0.7 42.9 %copy-start.35 = (bf16[1,2,24]{2,1,0:T(2,128)(2,1)S(1)}, bf16[1,2,24]{2,1,0:T(2,128)(2,1)}, u32[]{:S(2)}) copy-start(bf16[1,2,24]{2,1,0:T(2,128)(2,1)} %param.20) | copy-start | bytes 292
  0.7 42.9 %copy-start.32 = (s32[16]{0:T(128)S(1)}, s32[16]{0:T(128)}, u32[]{:S(2)}) copy-start(s32[16]{0:T(128)} %param.12) | copy-start | bytes 196
  1.7 17.4 %collective-permute-start = (bf16[1,2,96,768]{3,2,1,0:T(8,128)(2,1)S(1)}, bf16[1,2,96,768]{3,2,1,0:T(8,128)(2,1)S(1)}, u32[]{:S(2)}, u32[]{:S(2)}) collective-permute-start(bf16[1,2,96,768]{3,2,1,0:T(8,128)(2,1)S(1)} %maximum_bitcast_fusion.1), channel_id=1, source_target_pairs={{0,8},{1,9},{2,10},{3,11},{4,12},{5,13},{6,14},{7,15},{8,0},{9,1},... | collective-permute-start | bytes 884744 | tf_op jit(solution)/shard_map/ppermute | solution.py:49
  19.2 14.6 %collective-permute-start.1 = (bf16[2,2,96,768]{3,2,1,0:T(8,128)(2,1)S(1)}, bf16[2,2,96,768]{3,2,1,0:T(8,128)(2,1)S(1)}, u32[]{:S(2)}, u32[]{:S(2)}) collective-permute-start(bf16[2,2,96,768]{3,2,1,0:T(8,128)(2,1)S(1)} %pad_maximum_fusion.6), channel_id=1, source_target_pairs={{0,4},{1,5},{2,6},{3,7},{4,0},{5,1},{6,2},{7,3},{8,12},{9,13},{10,... | collective-permute-start | bytes 1769480 | tf_op jit(solution)/shard_map/ppermute | solution.py:49
  33.9 185.7 %copy-start.28 = (s32[16,64,2]{1,2,0:T(2,128)S(1)}, s32[16,64,2]{1,2,0:T(2,128)}, u32[]{:S(2)}) copy-start(s32[16,64,2]{1,2,0:T(2,128)} %param.14) | copy-start | bytes 24580
  33.9 197.0 %all-to-all-start = ((bf16[16,64,2,768]{3,2,1,0:T(2,128)(2,1)}), bf16[16,64,2,768]{3,2,1,0:T(2,128)(2,1)}, u32[]{:S(2)}, u32[]{:S(2)}) async-start(bf16[16,64,2,768]{3,2,1,0:T(2,128)(2,1)} %param.11), calls=%async_computation | async-start | bytes 6291456 | tf_op jit(solution)/shard_map/all_to_all | solution.py:112
  40.6 160.3 %collective-permute-start.5 = (f32[1,96]{1,0:T(1,128)S(1)}, f32[1,96]{1,0:T(1,128)S(1)}, u32[]{:S(2)}, u32[]{:S(2)}) collective-permute-start(f32[1,96]{1,0:T(1,128)S(1)} %convert_element_type.301), channel_id=1, source_target_pairs={{0,8},{1,9},{2,10},{3,11},{4,12},{5,13},{6,14},{7,15},{8,0},{9,1},... | collective-permute-start | bytes 1160 | tf_op jit(solution)/shard_map/ppermute | solution.py:49
  44.2 58.4 %collective-permute-start.2 = (bf16[4,2,96,768]{3,2,1,0:T(8,128)(2,1)S(1)}, bf16[4,2,96,768]{3,2,1,0:T(8,128)(2,1)S(1)}, u32[]{:S(2)}, u32[]{:S(2)}) collective-permute-start(bf16[4,2,96,768]{3,2,1,0:T(8,128)(2,1)S(1)} %pad_maximum_fusion.5), channel_id=1, source_target_pairs={{0,2},{1,3},{2,0},{3,1},{4,6},{5,7},{6,4},{7,5},{8,10},{9,11},{10,... | collective-permute-start | bytes 3538952 | tf_op jit(solution)/shard_map/ppermute | solution.py:49
  46.6 194.4 %copy-start.29 = (pred[32,64]{1,0:T(8,128)(4,1)}, pred[32,64]{1,0:T(8,128)(4,1)S(1)}, u32[]{:S(2)}) copy-start(pred[32,64]{1,0:T(8,128)(4,1)S(1)} %add_compare_fusion) | copy-start | bytes 6148
  104.3 119.2 %collective-permute-start.3 = (bf16[8,2,96,768]{3,2,1,0:T(8,128)(2,1)}, bf16[8,2,96,768]{3,2,1,0:T(8,128)(2,1)}, u32[]{:S(2)}, u32[]{:S(2)}) collective-permute-start(bf16[8,2,96,768]{3,2,1,0:T(8,128)(2,1)} %pad_maximum_fusion.2), channel_id=1, source_target_pairs={{0,16},{16,0},{1,17},{17,1},{2,18},{18,2},{3,19},{19,3},{4,20},{20... | collective-permute-start | bytes 7077896 | tf_op jit(solution)/shard_map/ppermute | solution.py:49
  200.9 10.0 %collective-permute-start.6 = (f32[2,96]{1,0:T(2,128)S(1)}, f32[2,96]{1,0:T(2,128)S(1)}, u32[]{:S(2)}, u32[]{:S(2)}) collective-permute-start(f32[2,96]{1,0:T(2,128)S(1)} %pad_maximum_fusion.10), channel_id=1, source_target_pairs={{0,4},{1,5},{2,6},{3,7},{4,0},{5,1},{6,2},{7,3},{8,12},{9,13},{10,... | collective-permute-start | bytes 2312 | tf_op jit(solution)/shard_map/ppermute | solution.py:49
  210.9 3.9 collective-permute-start.7
  214.8 3.7 collective-permute-start.8
  218.5 2.7 collective-permute-start.9
  227.2 41.2 %collective-permute-start.4 = (bf16[16,2,96,768]{3,2,1,0:T(8,128)(2,1)}, bf16[16,2,96,768]{3,2,1,0:T(8,128)(2,1)}, u32[]{:S(2)}, u32[]{:S(2)}) collective-permute-start(bf16[16,2,96,768]{3,2,1,0:T(8,128)(2,1)} %pad_maximum_fusion), channel_id=1, source_target_pairs={{0,1},{1,0},{2,3},{3,2},{4,5},{5,4},{6,7},{7,6},{8,9},{9,8},{10,11... | collective-permute-start | bytes 14155784 | tf_op jit(solution)/shard_map/ppermute | solution.py:49
  235.1 90.8 %all-to-all-start.2 = ((bf16[16,64,2,768]{3,2,1,0:T(2,128)(2,1)}), bf16[16,64,2,768]{3,2,1,0:T(2,128)(2,1)S(1)}, u32[]{:S(2)}, u32[]{:S(2)}) async-start(bf16[16,64,2,768]{3,2,1,0:T(2,128)(2,1)} %param.15), calls=%async_computation.2 | async-start | bytes 6291456 | tf_op jit(solution)/shard_map/all_to_all | solution.py:114
  338.3 59.0 %copy-start.2 = (f32[2048,768]{1,0:T(8,128)}, f32[2048,768]{1,0:T(8,128)S(1)}, u32[]{:S(2)}) copy-start(f32[2048,768]{1,0:T(8,128)S(1)} %get-tuple-element.63) | copy-start | bytes 18874372
  356.1 41.2 %slice-start.3 = ((s8[6291456]{0:T(1024)(128)(4,1)}), s8[2097152]{0:T(1024)(128)(4,1)S(1)}, s32[]{:S(2)}) async-start(s8[6291456]{0:T(1024)(128)(4,1)} %bitcast.143), calls=%async_computation.7 | async-start | bytes 4194304
  414.7 71.7 %all-to-all-start.1 = ((bf16[16,2,64,768]{3,1,2,0:T(2,128)(2,1)}), bf16[16,2,64,768]{3,1,2,0:T(2,128)(2,1)S(1)}, u32[]{:S(2)}, u32[]{:S(2)}) async-start(bf16[16,2,64,768]{3,1,2,0:T(2,128)(2,1)} %copy.55), calls=%async_computation.1 | async-start | bytes 6291456 | tf_op jit(solution)/shard_map/all_to_all | solution.py:136
  446.1 23.4 %collective-permute-start.15 = (bf16[16,96,768]{2,1,0:T(8,128)(2,1)}, bf16[16,96,768]{2,1,0:T(8,128)(2,1)}, u32[]{:S(2)}, u32[]{:S(2)}) collective-permute-start(bf16[16,96,768]{2,1,0:T(8,128)(2,1)} %bitcast.57), channel_id=1, source_target_pairs={{0,1},{1,0},{2,3},{3,2},{4,5},{5,4},{6,7},{7,6},{8,9},{9,8},{10,11... | collective-permute-start | bytes 7077896 | tf_op jit(solution)/shard_map/ppermute | solution.py:49
  446.6 27.6 %collective-permute-start.10 = (bf16[16,96,768]{2,1,0:T(8,128)(2,1)}, bf16[16,96,768]{2,1,0:T(8,128)(2,1)}, u32[]{:S(2)}, u32[]{:S(2)}) collective-permute-start(bf16[16,96,768]{2,1,0:T(8,128)(2,1)} %bitcast.47), channel_id=1, source_target_pairs={{0,1},{1,0},{2,3},{3,2},{4,5},{5,4},{6,7},{7,6},{8,9},{9,8},{10,11... | collective-permute-start | bytes 7077896 | tf_op jit(solution)/shard_map/ppermute | solution.py:49
  473.7 30.2 %collective-permute-start.16 = (bf16[8,96,768]{2,1,0:T(8,128)(2,1)}, bf16[8,96,768]{2,1,0:T(8,128)(2,1)}, u32[]{:S(2)}, u32[]{:S(2)}) collective-permute-start(bf16[8,96,768]{2,1,0:T(8,128)(2,1)} %slice.259), channel_id=1, source_target_pairs={{0,16},{16,0},{1,17},{17,1},{2,18},{18,2},{3,19},{19,3},{4,20},{20... | collective-permute-start | bytes 3538952 | tf_op jit(solution)/shard_map/ppermute | solution.py:49
  478.1 49.5 %collective-permute-start.11 = (bf16[8,96,768]{2,1,0:T(8,128)(2,1)}, bf16[8,96,768]{2,1,0:T(8,128)(2,1)}, u32[]{:S(2)}, u32[]{:S(2)}) collective-permute-start(bf16[8,96,768]{2,1,0:T(8,128)(2,1)} %slice.260), channel_id=1, source_target_pairs={{0,16},{16,0},{1,17},{17,1},{2,18},{18,2},{3,19},{19,3},{4,20},{20... | collective-permute-start | bytes 3538952 | tf_op jit(solution)/shard_map/ppermute | solution.py:49
  486.4 159.3 %all-to-all-start.3 = ((bf16[16,2,64,768]{3,1,2,0:T(2,128)(2,1)}), bf16[16,2,64,768]{3,1,2,0:T(2,128)(2,1)}, u32[]{:S(2)}, u32[]{:S(2)}) async-start(bf16[16,2,64,768]{3,1,2,0:T(2,128)(2,1)} %copy.60), calls=%async_computation.3 | async-start | bytes 6291456 | tf_op jit(solution)/shard_map/all_to_all | solution.py:168
  506.3 31.4 %collective-permute-start.17 = (bf16[4,96,768]{2,1,0:T(8,128)(2,1)S(1)}, bf16[4,96,768]{2,1,0:T(8,128)(2,1)S(1)}, u32[]{:S(2)}, u32[]{:S(2)}) collective-permute-start(bf16[4,96,768]{2,1,0:T(8,128)(2,1)S(1)} %slice.261), channel_id=1, source_target_pairs={{0,2},{1,3},{2,0},{3,1},{4,6},{5,7},{6,4},{7,5},{8,10},{9,11},{10,... | collective-permute-start | bytes 1769480 | tf_op jit(solution)/shard_map/ppermute | solution.py:49
  530.0 28.4 %collective-permute-start.12 = (bf16[4,96,768]{2,1,0:T(8,128)(2,1)S(1)}, bf16[4,96,768]{2,1,0:T(8,128)(2,1)S(1)}, u32[]{:S(2)}, u32[]{:S(2)}) collective-permute-start(bf16[4,96,768]{2,1,0:T(8,128)(2,1)S(1)} %slice.262), channel_id=1, source_target_pairs={{0,2},{1,3},{2,0},{3,1},{4,6},{5,7},{6,4},{7,5},{8,10},{9,11},{10,... | collective-permute-start | bytes 1769480 | tf_op jit(solution)/shard_map/ppermute | solution.py:49
  538.7 21.3 %collective-permute-start.18 = (bf16[2,96,768]{2,1,0:T(8,128)(2,1)}, bf16[2,96,768]{2,1,0:T(8,128)(2,1)}, u32[]{:S(2)}, u32[]{:S(2)}) collective-permute-start(bf16[2,96,768]{2,1,0:T(8,128)(2,1)} %slice.263), channel_id=1, source_target_pairs={{0,4},{1,5},{2,6},{3,7},{4,0},{5,1},{6,2},{7,3},{8,12},{9,13},{10,... | collective-permute-start | bytes 884744 | tf_op jit(solution)/shard_map/ppermute | solution.py:49
  559.6 8.9 %collective-permute-start.13 = (bf16[2,96,768]{2,1,0:T(8,128)(2,1)}, bf16[2,96,768]{2,1,0:T(8,128)(2,1)}, u32[]{:S(2)}, u32[]{:S(2)}) collective-permute-start(bf16[2,96,768]{2,1,0:T(8,128)(2,1)} %slice.264), channel_id=1, source_target_pairs={{0,4},{1,5},{2,6},{3,7},{4,0},{5,1},{6,2},{7,3},{8,12},{9,13},{10,... | collective-permute-start | bytes 884744 | tf_op jit(solution)/shard_map/ppermute | solution.py:49
  561.2 17.0 %collective-permute-start.19 = (bf16[1,96,768]{2,1,0:T(8,128)(2,1)S(1)}, bf16[1,96,768]{2,1,0:T(8,128)(2,1)S(1)}, u32[]{:S(2)}, u32[]{:S(2)}) collective-permute-start(bf16[1,96,768]{2,1,0:T(8,128)(2,1)S(1)} %slice.265), channel_id=1, source_target_pairs={{0,8},{1,9},{2,10},{3,11},{4,12},{5,13},{6,14},{7,15},{8,0},{9,1},... | collective-permute-start | bytes 442376 | tf_op jit(solution)/shard_map/ppermute | solution.py:49
  569.7 15.6 %collective-permute-start.14 = (bf16[1,96,768]{2,1,0:T(8,128)(2,1)S(1)}, bf16[1,96,768]{2,1,0:T(8,128)(2,1)S(1)}, u32[]{:S(2)}, u32[]{:S(2)}) collective-permute-start(bf16[1,96,768]{2,1,0:T(8,128)(2,1)S(1)} %slice.266), channel_id=1, source_target_pairs={{0,8},{1,9},{2,10},{3,11},{4,12},{5,13},{6,14},{7,15},{8,0},{9,1},... | collective-permute-start | bytes 442376 | tf_op jit(solution)/shard_map/ppermute | solution.py:49
  (40 other events, 546.8 us)
where the time goes:
time: 663 us; the launch traced here: 657 us
  matrix products  148 us (22%)
  waiting for transfers between devices  143 us (22%)
  blocking collectives  123 us (19%)
  other arithmetic  103 us (16%)
  local copies, waits for them, and re-layouts  74.2 us (11%)
  starting transfers between devices  59.6 us (9%)
    ppermute x20, waiting for transfers between devices, swap(): return lax.ppermute(values, axis, [(i, i ^ mask) for i in range(size)])  143 us
    unnamed x1, blocking collectives  83.7 us
    psum x1, blocking collectives, body(): rest = lax.psum(rest, ('batch', 'seq'))  39.5 us
    dot_general x1, matrix products, body(): jnp.einsum('td,fd->tf', summed_low, w_second, preferred_element_type=F32)  34.4 us
    ppermute x20, starting transfers between devices, swap(): return lax.ppermute(values, axis, [(i, i ^ mask) for i in range(size)])  30.7 us
    dot_general x1, matrix products, body(): jnp.einsum('td,fd->tf', normed_low, w_first, preferred_element_type=F32)  24.9 us
    unnamed x100, local copies, waits for them, and re-layouts  18.2 us
    dot_general x1, matrix products, body(): jnp.einsum('tf,td->fd', act_low, summed_low, preferred_element_type=F32)  17.8 us
  transfers between devices with their start and end apart: 24, of which 10 were waited for; matrix products, arithmetic and copies ran while one was open for 34% of the time, Pallas kernels for 0%

commit v1 on v0

--- a/solution.py
+++ b/solution.py
@@ -208,7 +208,8 @@
             sums,
         ]
     )
-    rest = lax.psum(rest, ("batch", "seq"))
+    for mesh_axis in ("seq", "batch"):
+        rest = lax.psum(rest, mesh_axis)
     slice_of = D // (lax.axis_size("batch") * groups)
     norms = lax.dynamic_slice_in_dim(rest[:5], here * slice_of, slice_of, axis=1)
     grad_b_in = lax.dynamic_slice_in_dim(rest[5:-1].reshape(-1), here * share, share, axis=0)

time: 663 us -> 689 us (1.039)
  blocking collectives: 123 us -> 149 us
    psum x1 -> x2, blocking collectives: 39.5 us -> 65.6 us  [body(): rest = lax.psum(rest, mesh_axis)]
  transfers between devices with their start and end apart: 24 -> 24, of which waited for: 10 -> 10; matrix products, arithmetic and copies ran while one was open for 34% -> 33% of each run, Pallas kernels for 0% -> 0%
where the time goes in v1:
time: 689 us; the launch traced here: 683 us
  blocking collectives  149 us (22%)
  matrix products  148 us (21%)
  waiting for transfers between devices  143 us (21%)
  other arithmetic  103 us (15%)
  local copies, waits for them, and re-layouts  74.2 us (11%)
  starting transfers between devices  59.5 us (9%)
    ppermute x20, waiting for transfers between devices, swap(): return lax.ppermute(values, axis, [(i, i ^ mask) for i in range(size)])  143 us
    unnamed x1, blocking collectives  83.7 us
    psum x2, blocking collectives, body(): rest = lax.psum(rest, mesh_axis)  65.6 us
    dot_general x1, matrix products, body(): jnp.einsum('td,fd->tf', summed_low, w_second, preferred_element_type=F32)  34.4 us
    ppermute x20, starting transfers between devices, swap(): return lax.ppermute(values, axis, [(i, i ^ mask) for i in range(size)])  30.7 us
    dot_general x1, matrix products, body(): jnp.einsum('td,fd->tf', normed_low, w_first, preferred_element_type=F32)  24.9 us
    unnamed x100, local copies, waits for them, and re-layouts  18.2 us
    dot_general x1, matrix products, body(): jnp.einsum('tf,td->fd', act_low, summed_low, preferred_element_type=F32)  17.8 us
  transfers between devices with their start and end apart: 24, of which 10 were waited for; matrix products, arithmetic and copies ran while one was open for 33% of the time, Pallas kernels for 0%

profile of v1, /device:TPU:0, one launch (start us, length us, event | category | flops | bytes accessed | tf_op | source)
XLA Modules:
  0.0 682.6 jit_solution(4382830192867453282)
XLA Ops:
  5.8 13.3 %collective-permute-done = bf16[1,2,96,768]{3,2,1,0:T(8,128)(2,1)S(1)} collective-permute-done((bf16[1,2,96,768]{3,2,1,0:T(8,128)(2,1)S(1)}, bf16[1,2,96,768]{3,2,1,0:T(8,128)(2,1)S(1)}, u32[]{:S(2)}, u32[]{:S(2)}) %collective-permute-start) | collective-permute-done | bytes 294944 | tf_op jit(solution)/shard_map/ppermute | solution.py:49
  20.0 13.8 %collective-permute-done.1 = bf16[2,2,96,768]{3,2,1,0:T(8,128)(2,1)S(1)} collective-permute-done((bf16[2,2,96,768]{3,2,1,0:T(8,128)(2,1)S(1)}, bf16[2,2,96,768]{3,2,1,0:T(8,128)(2,1)S(1)}, u32[]{:S(2)}, u32[]{:S(2)}) %collective-permute-start.1) | collective-permute-done | bytes 589856 | tf_op jit(solution)/shard_map/ppermute | solution.py:49
  33.9 6.6 all-to-all-start
  47.2 55.5 %collective-permute-done.2 = bf16[4,2,96,768]{3,2,1,0:T(8,128)(2,1)S(1)} collective-permute-done((bf16[4,2,96,768]{3,2,1,0:T(8,128)(2,1)S(1)}, bf16[4,2,96,768]{3,2,1,0:T(8,128)(2,1)S(1)}, u32[]{:S(2)}, u32[]{:S(2)}) %collective-permute-start.2) | collective-permute-done | bytes 1179680 | tf_op jit(solution)/shard_map/ppermute | solution.py:49
  106.1 83.7 %all-reduce.1 = bf16[3840]{0:T(1024)(128)(2,1)S(1)} all-reduce(bf16[3840]{0:T(1024)(128)(2,1)S(1)} %dynamic-update-slice), channel_id=2, replica_groups=mesh['batch'=2,'seq'=16] {'batch','seq'}, use_global_device_ids=true, to_apply=%add.1 | all-reduce | flops 3840 | bytes 15360
  190.8 10.0 %fusion.34 = bf16[1,768,768]{2,1,0:T(8,128)(2,1)} fusion(), kind=kLoop, calls=%fused_computation.87 | loop fusion | flops 8257536 | bytes 1179648 | tf_op jit(solution)/shard_map/neg | solution.py:110
  200.9 9.9 %multiply_convert_fusion.2 = bf16[1,768,768]{2,1,0:T(8,128)(2,1)} fusion(), kind=kLoop, calls=%fused_computation.82 | loop fusion | flops 6488064 | bytes 1179648 | tf_op jit(solution)/shard_map/convert_element_type | solution.py:36
  235.1 5.8 all-to-all-start.2
  252.6 7.2 %fusion.73 = (f32[32,64]{1,0:T(8,128)S(1)}, f32[32,64,768]{2,1,0:T(8,128)}) fusion(bf16[32,2,64,768]{3,2,1,0:T(8,128)(2,1)S(1)} %bitcast.161, bf16[1,768,768]{2,1,0:T(8,128)(2,1)S(1)} %copy-done.10, bf16[1,768,768]{2,1,0:T(8,128)(2,1)S(1)} %copy-done.12, bf16[32,64,768]{2,1,0:T(8,128)(2,1)S(1)} %bitcast_select_fusion), kind=kOutput, calls=%fused_computation.198 | convolution fusion | flops 4837734400 | bytes 18096128 | tf_op jit(solution)/shard_map/lund,ude->lne/dot_general | solution.py:127
  268.4 4.9 constant_dynamic-update-slice_fusion
  273.3 8.0 %fusion.70 = (bf16[32,1,96,768]{3,2,1,0:T(8,128)(2,1)}, bf16[32,1,96,768]{3,2,1,0:T(8,128)(2,1)}) fusion(bf16[32,2,96,768]{3,2,1,0:T(8,128)(2,1)} %constant_dynamic-update-slice_fusion), kind=kLoop, calls=%fused_computation.195 | loop fusion | bytes 18874368 | tf_op jit(solution)/shard_map/slice | solution.py:96
  281.3 24.9 %multiply_convert_fusion = (bf16[2048,3072]{1,0:T(8,128)(2,1)}, f32[2048,3072]{1,0:T(8,128)}) fusion(f32[3072]{0:T(1024)S(1)} %add.305, bf16[2048,768]{1,0:T(8,128)(2,1)} %bitcast.169, bf16[3072,768]{1,0:T(8,128)(2,1)} %bitcast.162), kind=kOutput, calls=%fused_computation.9 | convolution fusion | flops 9726590976 | bytes 45625344 | tf_op jit(solution)/shard_map/td,fd->tf/dot_general | solution.py:131
  306.2 16.2 %fusion.74 = (f32[2048]{0:T(1024)S(1)}, f32[2048,768]{1,0:T(8,128)S(1)}) fusion(f32[768]{0:T(1024)S(1)} %add.311, bf16[2048,3072]{1,0:T(8,128)(2,1)} %get-tuple-element.82, bf16[3072,768]{1,0:T(8,128)(2,1)} %bitcast.164, f32[768]{0:T(1024)S(1)} %add.300, f32[768]{0:T(1024)S(1)} %mul.622, f32[2048]{0:T(1024)S(1)} %rsqrt.25, f32[2048]{0:T(1024)S(1)} %div.52, ...), kind=kOutput, calls=%fused_computation.199 | convolution fusion | flops 9674684416 | bytes 29918208 | tf_op jit(solution)/shard_map/dot_general | solution.py:133
  338.3 17.8 %fusion.67 = f32[3072,768]{1,0:T(8,128)} fusion(bf16[2048,3072]{1,0:T(8,128)(2,1)} %get-tuple-element.82, f32[2048,768]{1,0:T(8,128)S(1)} %get-tuple-element.63, f32[2048]{0:T(1024)S(1)} %negate_multiply_fusion.1), kind=kOutput, calls=%fused_computation.192 | convolution fusion | flops 9666822144 | bytes 28319744 | tf_op jit(solution)/shard_map/tf,td->fd/dot_general | solution.py:143
  356.1 34.4 %fusion.75 = (f32[3072]{0:T(1024)S(1)}, bf16[2048,3072]{1,0:T(8,128)(2,1)}) fusion(bf16[3072,768]{1,0:T(8,128)(2,1)} %bitcast.165, f32[2048,768]{1,0:T(8,128)S(1)} %get-tuple-element.63, f32[2048]{0:T(1024)S(1)} %negate_multiply_fusion.1, f32[2048,3072]{1,0:T(8,128)} %get-tuple-element.83, f32[3072]{0:T(1024)S(1)} %add.305), kind=kOutput, calls=%fused_computation.200 | convolution fusion | flops 9830396928 | bytes 48791552 | tf_op jit(solution)/shard_map/td,fd->tf/dot_general | solution.py:144
  390.5 6.8 copy.55
  397.3 17.3 %multiply_reduce_fusion = (f32[768]{0:T(1024)S(1)}, f32[2048]{0:T(1024)S(1)}, f32[768]{0:T(1024)S(1)}, f32[2048,768]{1,0:T(8,128)}) fusion(f32[32,64,768]{2,1,0:T(8,128)S(1)} %bitcast.144, f32[2048]{0:T(1024)S(1)} %rsqrt.25, f32[2048]{0:T(1024)S(1)} %div.52, f32[768]{0:T(1024)S(1)} %mul.622, bf16[3072,768]{1,0:T(8,128)(2,1)} %bitcast.163, ...), kind=kOutput, calls=%fused_computation.39 | convolution fusion | flops 9679400960 | bytes 36217856 | tf_op jit(solution)/shard_map/dot_general | solution.py:150
  414.7 6.5 all-to-all-start.1
  421.2 7.2 %fusion.68 = (f32[2048]{0:T(1024)S(1)}, f32[2048,768]{1,0:T(8,128)S(1)}, bf16[2048,768]{1,0:T(8,128)(2,1)}) fusion(f32[2048]{0:T(1024)S(1)} %multiply_multiply_fusion.2, f32[2048]{0:T(1024)S(1)} %div.52, f32[32,64,768]{2,1,0:T(8,128)} %get-tuple-element.81, f32[2048]{0:T(1024)S(1)} %rsqrt.25, f32[2048,768]{1,0:T(8,128)} %get-tuple-element.86, ...), kind=kLoop, calls=%fused_computation.193 | loop fusion | flops 17299456 | bytes 22059008 | tf_op jit(solution)/shard_map/transpose(jvp())/reduce_sum | solution.py:18
  428.4 14.2 %fusion.17 = f32[3072,768]{1,0:T(8,128)S(1)} fusion(bf16[2048,768]{1,0:T(8,128)(2,1)} %get-tuple-element.70, bf16[2048,3072]{1,0:T(8,128)(2,1)} %get-tuple-element.88), kind=kOutput, calls=%fused_computation.43 | convolution fusion | flops 9663676416 | bytes 25165824 | tf_op jit(solution)/shard_map/tf,td->fd/dot_general | solution.py:149
  448.9 8.9 %convert_bitcast_fusion.1 = bf16[32,2,64,768]{3,2,0,1:T(8,128)(2,1)} fusion(bf16[32,64,768,1]{2,1,0,3:T(8,128)(2,1)} %bitcast.167, bf16[1,768,768]{2,1,0:T(8,128)(2,1)S(1)} %copy-done.11, bf16[1,768,768]{2,1,0:T(8,128)(2,1)} %multiply_convert_fusion.2), kind=kOutput, calls=%fused_computation.40 | convolution fusion | flops 4839702528 | bytes 11796480 | tf_op jit(solution)/shard_map/lne,ude->lund/dot_general | solution.py:154
  486.4 9.8 %all-to-all-start.3 = ((bf16[16,2,64,768]{3,1,2,0:T(2,128)(2,1)}), bf16[16,2,64,768]{3,1,2,0:T(2,128)(2,1)}, u32[]{:S(2)}, u32[]{:S(2)}) async-start(bf16[16,2,64,768]{3,1,2,0:T(2,128)(2,1)} %copy.60), calls=%async_computation.3 | async-start | bytes 6291456 | tf_op jit(solution)/shard_map/all_to_all | solution.py:168
  508.4 19.3 %collective-permute-done.11 = bf16[8,96,768]{2,1,0:T(8,128)(2,1)} collective-permute-done((bf16[8,96,768]{2,1,0:T(8,128)(2,1)}, bf16[8,96,768]{2,1,0:T(8,128)(2,1)}, u32[]{:S(2)}, u32[]{:S(2)}) %collective-permute-start.11) | collective-permute-done | bytes 1179680 | tf_op jit(solution)/shard_map/ppermute | solution.py:49
  532.2 5.6 collective-permute-done.17
  538.7 19.7 %collective-permute-done.12 = bf16[4,96,768]{2,1,0:T(8,128)(2,1)S(1)} collective-permute-done((bf16[4,96,768]{2,1,0:T(8,128)(2,1)S(1)}, bf16[4,96,768]{2,1,0:T(8,128)(2,1)S(1)}, u32[]{:S(2)}, u32[]{:S(2)}) %collective-permute-start.12) | collective-permute-done | bytes 589856 | tf_op jit(solution)/shard_map/ppermute | solution.py:49
  561.3 7.2 %collective-permute-done.13 = bf16[2,96,768]{2,1,0:T(8,128)(2,1)} collective-permute-done((bf16[2,96,768]{2,1,0:T(8,128)(2,1)}, bf16[2,96,768]{2,1,0:T(8,128)(2,1)}, u32[]{:S(2)}, u32[]{:S(2)}) %collective-permute-start.13) | collective-permute-done | bytes 294944 | tf_op jit(solution)/shard_map/ppermute | solution.py:49
  569.7 8.5 %collective-permute-start.14 = (bf16[1,96,768]{2,1,0:T(8,128)(2,1)S(1)}, bf16[1,96,768]{2,1,0:T(8,128)(2,1)S(1)}, u32[]{:S(2)}, u32[]{:S(2)}) collective-permute-start(bf16[1,96,768]{2,1,0:T(8,128)(2,1)S(1)} %slice.266), channel_id=1, source_target_pairs={{0,8},{1,9},{2,10},{3,11},{4,12},{5,13},{6,14},{7,15},{8,0},{9,1},... | collective-permute-start | bytes 442376 | tf_op jit(solution)/shard_map/ppermute | solution.py:49
  579.0 6.4 collective-permute-done.14
  588.7 13.2 %fusion.22 = (f32[16,2,64]{1,2,0:T(8,128)S(1)}, f32[16,2,64]{1,2,0:T(8,128)S(1)}) fusion(bf16[16,2,64,768]{3,1,2,0:T(2,128)(2,1)S(1)} %all-to-all-done.1, f32[16,2,64]{1,2,0:T(8,128)S(1)} %reduce_max.15, s32[16,2,64]{1,2,0:T(8,128)} %copy.62), kind=kLoop, calls=%fused_computation.60 | loop fusion | flops 9433088 | bytes 3178496 | tf_op jit(solution)/shard_map/reduce_sum | solution.py:195
  604.3 57.7 %psum.14 = f32[10,768]{1,0:T(8,128)S(1)} all-reduce(f32[10,768]{1,0:T(8,128)S(1)} %concatenate.64), channel_id=1, replica_groups=mesh['batch'=2,'seq'=16] {'seq'}, use_global_device_ids=true, to_apply=%region_20.21 | all-reduce | flops 7680 | bytes 61440 | tf_op jit(solution)/shard_map/psum | solution.py:212
  662.0 7.9 %psum.15 = f32[10,768]{1,0:T(8,128)S(1)} all-reduce(f32[10,768]{1,0:T(8,128)S(1)} %psum.14), channel_id=1, replica_groups=mesh['batch'=2,'seq'=16] {'batch'}, use_global_device_ids=true, to_apply=%region_21.22 | all-reduce | flops 7680 | bytes 61440 | tf_op jit(solution)/shard_map/psum | solution.py:212
  675.4 5.9 copy.77
  (265 shorter events, 144.0 us)
Async XLA Ops:
  0.6 45.3 %copy-start.36 = (s32[32]{0:T(128)S(1)}, s32[32]{0:T(128)}, u32[]{:S(2)}) copy-start(s32[32]{0:T(128)} %constant.129.clone) | copy-start | bytes 388
  0.7 42.8 %copy-start.34 = (bf16[1,3,24]{2,1,0:T(4,128)(2,1)S(1)}, bf16[1,3,24]{2,1,0:T(4,128)(2,1)}, u32[]{:S(2)}) copy-start(bf16[1,3,24]{2,1,0:T(4,128)(2,1)} %param.19) | copy-start | bytes 436
  0.7 42.9 %copy-start.35 = (bf16[1,2,24]{2,1,0:T(2,128)(2,1)S(1)}, bf16[1,2,24]{2,1,0:T(2,128)(2,1)}, u32[]{:S(2)}) copy-start(bf16[1,2,24]{2,1,0:T(2,128)(2,1)} %param.20) | copy-start | bytes 292
  0.7 42.9 %copy-start.32 = (s32[16]{0:T(128)S(1)}, s32[16]{0:T(128)}, u32[]{:S(2)}) copy-start(s32[16]{0:T(128)} %param.12) | copy-start | bytes 196
  1.7 17.4 %collective-permute-start = (bf16[1,2,96,768]{3,2,1,0:T(8,128)(2,1)S(1)}, bf16[1,2,96,768]{3,2,1,0:T(8,128)(2,1)S(1)}, u32[]{:S(2)}, u32[]{:S(2)}) collective-permute-start(bf16[1,2,96,768]{3,2,1,0:T(8,128)(2,1)S(1)} %maximum_bitcast_fusion.1), channel_id=1, source_target_pairs={{0,8},{1,9},{2,10},{3,11},{4,12},{5,13},{6,14},{7,15},{8,0},{9,1},... | collective-permute-start | bytes 884744 | tf_op jit(solution)/shard_map/ppermute | solution.py:49
  19.2 14.6 %collective-permute-start.1 = (bf16[2,2,96,768]{3,2,1,0:T(8,128)(2,1)S(1)}, bf16[2,2,96,768]{3,2,1,0:T(8,128)(2,1)S(1)}, u32[]{:S(2)}, u32[]{:S(2)}) collective-permute-start(bf16[2,2,96,768]{3,2,1,0:T(8,128)(2,1)S(1)} %pad_maximum_fusion.6), channel_id=1, source_target_pairs={{0,4},{1,5},{2,6},{3,7},{4,0},{5,1},{6,2},{7,3},{8,12},{9,13},{10,... | collective-permute-start | bytes 1769480 | tf_op jit(solution)/shard_map/ppermute | solution.py:49
  33.9 185.7 %copy-start.28 = (s32[16,64,2]{1,2,0:T(2,128)S(1)}, s32[16,64,2]{1,2,0:T(2,128)}, u32[]{:S(2)}) copy-start(s32[16,64,2]{1,2,0:T(2,128)} %param.14) | copy-start | bytes 24580
  33.9 196.9 %all-to-all-start = ((bf16[16,64,2,768]{3,2,1,0:T(2,128)(2,1)}), bf16[16,64,2,768]{3,2,1,0:T(2,128)(2,1)}, u32[]{:S(2)}, u32[]{:S(2)}) async-start(bf16[16,64,2,768]{3,2,1,0:T(2,128)(2,1)} %param.11), calls=%async_computation | async-start | bytes 6291456 | tf_op jit(solution)/shard_map/all_to_all | solution.py:112
  40.6 160.3 %collective-permute-start.5 = (f32[1,96]{1,0:T(1,128)S(1)}, f32[1,96]{1,0:T(1,128)S(1)}, u32[]{:S(2)}, u32[]{:S(2)}) collective-permute-start(f32[1,96]{1,0:T(1,128)S(1)} %convert_element_type.301), channel_id=1, source_target_pairs={{0,8},{1,9},{2,10},{3,11},{4,12},{5,13},{6,14},{7,15},{8,0},{9,1},... | collective-permute-start | bytes 1160 | tf_op jit(solution)/shard_map/ppermute | solution.py:49
  44.2 58.4 %collective-permute-start.2 = (bf16[4,2,96,768]{3,2,1,0:T(8,128)(2,1)S(1)}, bf16[4,2,96,768]{3,2,1,0:T(8,128)(2,1)S(1)}, u32[]{:S(2)}, u32[]{:S(2)}) collective-permute-start(bf16[4,2,96,768]{3,2,1,0:T(8,128)(2,1)S(1)} %pad_maximum_fusion.5), channel_id=1, source_target_pairs={{0,2},{1,3},{2,0},{3,1},{4,6},{5,7},{6,4},{7,5},{8,10},{9,11},{10,... | collective-permute-start | bytes 3538952 | tf_op jit(solution)/shard_map/ppermute | solution.py:49
  46.6 194.3 %copy-start.29 = (pred[32,64]{1,0:T(8,128)(4,1)}, pred[32,64]{1,0:T(8,128)(4,1)S(1)}, u32[]{:S(2)}) copy-start(pred[32,64]{1,0:T(8,128)(4,1)S(1)} %add_compare_fusion) | copy-start | bytes 6148
  104.3 119.2 %collective-permute-start.3 = (bf16[8,2,96,768]{3,2,1,0:T(8,128)(2,1)}, bf16[8,2,96,768]{3,2,1,0:T(8,128)(2,1)}, u32[]{:S(2)}, u32[]{:S(2)}) collective-permute-start(bf16[8,2,96,768]{3,2,1,0:T(8,128)(2,1)} %pad_maximum_fusion.2), channel_id=1, source_target_pairs={{0,16},{16,0},{1,17},{17,1},{2,18},{18,2},{3,19},{19,3},{4,20},{20... | collective-permute-start | bytes 7077896 | tf_op jit(solution)/shard_map/ppermute | solution.py:49
  200.9 10.0 %collective-permute-start.6 = (f32[2,96]{1,0:T(2,128)S(1)}, f32[2,96]{1,0:T(2,128)S(1)}, u32[]{:S(2)}, u32[]{:S(2)}) collective-permute-start(f32[2,96]{1,0:T(2,128)S(1)} %pad_maximum_fusion.10), channel_id=1, source_target_pairs={{0,4},{1,5},{2,6},{3,7},{4,0},{5,1},{6,2},{7,3},{8,12},{9,13},{10,... | collective-permute-start | bytes 2312 | tf_op jit(solution)/shard_map/ppermute | solution.py:49
  210.9 3.9 collective-permute-start.7
  214.8 3.7 collective-permute-start.8
  218.5 2.6 collective-permute-start.9
  227.1 41.2 %collective-permute-start.4 = (bf16[16,2,96,768]{3,2,1,0:T(8,128)(2,1)}, bf16[16,2,96,768]{3,2,1,0:T(8,128)(2,1)}, u32[]{:S(2)}, u32[]{:S(2)}) collective-permute-start(bf16[16,2,96,768]{3,2,1,0:T(8,128)(2,1)} %pad_maximum_fusion), channel_id=1, source_target_pairs={{0,1},{1,0},{2,3},{3,2},{4,5},{5,4},{6,7},{7,6},{8,9},{9,8},{10,11... | collective-permute-start | bytes 14155784 | tf_op jit(solution)/shard_map/ppermute | solution.py:49
  235.1 90.9 %all-to-all-start.2 = ((bf16[16,64,2,768]{3,2,1,0:T(2,128)(2,1)}), bf16[16,64,2,768]{3,2,1,0:T(2,128)(2,1)S(1)}, u32[]{:S(2)}, u32[]{:S(2)}) async-start(bf16[16,64,2,768]{3,2,1,0:T(2,128)(2,1)} %param.15), calls=%async_computation.2 | async-start | bytes 6291456 | tf_op jit(solution)/shard_map/all_to_all | solution.py:114
  338.3 59.0 %copy-start.2 = (f32[2048,768]{1,0:T(8,128)}, f32[2048,768]{1,0:T(8,128)S(1)}, u32[]{:S(2)}) copy-start(f32[2048,768]{1,0:T(8,128)S(1)} %get-tuple-element.63) | copy-start | bytes 18874372
  356.1 41.2 %slice-start.3 = ((s8[6291456]{0:T(1024)(128)(4,1)}), s8[2097152]{0:T(1024)(128)(4,1)S(1)}, s32[]{:S(2)}) async-start(s8[6291456]{0:T(1024)(128)(4,1)} %bitcast.143), calls=%async_computation.7 | async-start | bytes 4194304
  414.7 71.7 %all-to-all-start.1 = ((bf16[16,2,64,768]{3,1,2,0:T(2,128)(2,1)}), bf16[16,2,64,768]{3,1,2,0:T(2,128)(2,1)S(1)}, u32[]{:S(2)}, u32[]{:S(2)}) async-start(bf16[16,2,64,768]{3,1,2,0:T(2,128)(2,1)} %copy.55), calls=%async_computation.1 | async-start | bytes 6291456 | tf_op jit(solution)/shard_map/all_to_all | solution.py:136
  446.1 23.5 %collective-permute-start.15 = (bf16[16,96,768]{2,1,0:T(8,128)(2,1)}, bf16[16,96,768]{2,1,0:T(8,128)(2,1)}, u32[]{:S(2)}, u32[]{:S(2)}) collective-permute-start(bf16[16,96,768]{2,1,0:T(8,128)(2,1)} %bitcast.57), channel_id=1, source_target_pairs={{0,1},{1,0},{2,3},{3,2},{4,5},{5,4},{6,7},{7,6},{8,9},{9,8},{10,11... | collective-permute-start | bytes 7077896 | tf_op jit(solution)/shard_map/ppermute | solution.py:49
  446.6 27.7 %collective-permute-start.10 = (bf16[16,96,768]{2,1,0:T(8,128)(2,1)}, bf16[16,96,768]{2,1,0:T(8,128)(2,1)}, u32[]{:S(2)}, u32[]{:S(2)}) collective-permute-start(bf16[16,96,768]{2,1,0:T(8,128)(2,1)} %bitcast.47), channel_id=1, source_target_pairs={{0,1},{1,0},{2,3},{3,2},{4,5},{5,4},{6,7},{7,6},{8,9},{9,8},{10,11... | collective-permute-start | bytes 7077896 | tf_op jit(solution)/shard_map/ppermute | solution.py:49
  473.7 30.2 %collective-permute-start.16 = (bf16[8,96,768]{2,1,0:T(8,128)(2,1)}, bf16[8,96,768]{2,1,0:T(8,128)(2,1)}, u32[]{:S(2)}, u32[]{:S(2)}) collective-permute-start(bf16[8,96,768]{2,1,0:T(8,128)(2,1)} %slice.259), channel_id=1, source_target_pairs={{0,16},{16,0},{1,17},{17,1},{2,18},{18,2},{3,19},{19,3},{4,20},{20... | collective-permute-start | bytes 3538952 | tf_op jit(solution)/shard_map/ppermute | solution.py:49
  478.2 49.5 %collective-permute-start.11 = (bf16[8,96,768]{2,1,0:T(8,128)(2,1)}, bf16[8,96,768]{2,1,0:T(8,128)(2,1)}, u32[]{:S(2)}, u32[]{:S(2)}) collective-permute-start(bf16[8,96,768]{2,1,0:T(8,128)(2,1)} %slice.260), channel_id=1, source_target_pairs={{0,16},{16,0},{1,17},{17,1},{2,18},{18,2},{3,19},{19,3},{4,20},{20... | collective-permute-start | bytes 3538952 | tf_op jit(solution)/shard_map/ppermute | solution.py:49
  486.4 185.4 %all-to-all-start.3 = ((bf16[16,2,64,768]{3,1,2,0:T(2,128)(2,1)}), bf16[16,2,64,768]{3,1,2,0:T(2,128)(2,1)}, u32[]{:S(2)}, u32[]{:S(2)}) async-start(bf16[16,2,64,768]{3,1,2,0:T(2,128)(2,1)} %copy.60), calls=%async_computation.3 | async-start | bytes 6291456 | tf_op jit(solution)/shard_map/all_to_all | solution.py:168
  506.3 31.5 %collective-permute-start.17 = (bf16[4,96,768]{2,1,0:T(8,128)(2,1)S(1)}, bf16[4,96,768]{2,1,0:T(8,128)(2,1)S(1)}, u32[]{:S(2)}, u32[]{:S(2)}) collective-permute-start(bf16[4,96,768]{2,1,0:T(8,128)(2,1)S(1)} %slice.261), channel_id=1, source_target_pairs={{0,2},{1,3},{2,0},{3,1},{4,6},{5,7},{6,4},{7,5},{8,10},{9,11},{10,... | collective-permute-start | bytes 1769480 | tf_op jit(solution)/shard_map/ppermute | solution.py:49
  529.9 28.4 %collective-permute-start.12 = (bf16[4,96,768]{2,1,0:T(8,128)(2,1)S(1)}, bf16[4,96,768]{2,1,0:T(8,128)(2,1)S(1)}, u32[]{:S(2)}, u32[]{:S(2)}) collective-permute-start(bf16[4,96,768]{2,1,0:T(8,128)(2,1)S(1)} %slice.262), channel_id=1, source_target_pairs={{0,2},{1,3},{2,0},{3,1},{4,6},{5,7},{6,4},{7,5},{8,10},{9,11},{10,... | collective-permute-start | bytes 1769480 | tf_op jit(solution)/shard_map/ppermute | solution.py:49
  538.7 21.3 %collective-permute-start.18 = (bf16[2,96,768]{2,1,0:T(8,128)(2,1)}, bf16[2,96,768]{2,1,0:T(8,128)(2,1)}, u32[]{:S(2)}, u32[]{:S(2)}) collective-permute-start(bf16[2,96,768]{2,1,0:T(8,128)(2,1)} %slice.263), channel_id=1, source_target_pairs={{0,4},{1,5},{2,6},{3,7},{4,0},{5,1},{6,2},{7,3},{8,12},{9,13},{10,... | collective-permute-start | bytes 884744 | tf_op jit(solution)/shard_map/ppermute | solution.py:49
  559.6 8.9 %collective-permute-start.13 = (bf16[2,96,768]{2,1,0:T(8,128)(2,1)}, bf16[2,96,768]{2,1,0:T(8,128)(2,1)}, u32[]{:S(2)}, u32[]{:S(2)}) collective-permute-start(bf16[2,96,768]{2,1,0:T(8,128)(2,1)} %slice.264), channel_id=1, source_target_pairs={{0,4},{1,5},{2,6},{3,7},{4,0},{5,1},{6,2},{7,3},{8,12},{9,13},{10,... | collective-permute-start | bytes 884744 | tf_op jit(solution)/shard_map/ppermute | solution.py:49
  561.2 17.0 %collective-permute-start.19 = (bf16[1,96,768]{2,1,0:T(8,128)(2,1)S(1)}, bf16[1,96,768]{2,1,0:T(8,128)(2,1)S(1)}, u32[]{:S(2)}, u32[]{:S(2)}) collective-permute-start(bf16[1,96,768]{2,1,0:T(8,128)(2,1)S(1)} %slice.265), channel_id=1, source_target_pairs={{0,8},{1,9},{2,10},{3,11},{4,12},{5,13},{6,14},{7,15},{8,0},{9,1},... | collective-permute-start | bytes 442376 | tf_op jit(solution)/shard_map/ppermute | solution.py:49
  569.7 15.6 %collective-permute-start.14 = (bf16[1,96,768]{2,1,0:T(8,128)(2,1)S(1)}, bf16[1,96,768]{2,1,0:T(8,128)(2,1)S(1)}, u32[]{:S(2)}, u32[]{:S(2)}) collective-permute-start(bf16[1,96,768]{2,1,0:T(8,128)(2,1)S(1)} %slice.266), channel_id=1, source_target_pairs={{0,8},{1,9},{2,10},{3,11},{4,12},{5,13},{6,14},{7,15},{8,0},{9,1},... | collective-permute-start | bytes 442376 | tf_op jit(solution)/shard_map/ppermute | solution.py:49
  (40 other events, 546.6 us)
